TPU v7x, 32 devices: a whole 2x2x4 slice. The times are simulated.
32 devices in a mesh: dp: 2 (over y), expert: 16 (over z, x, core).
Axes of the slice: x: 2, y: 2, z: 4, core: 2. Of those that a mesh axis runs over, the one named last changes fastest.
Arguments:
- tokens: bfloat16 [2048, 3584], P('expert', 'dp'), may hold values from -6 to 6
- expert_ids: int32 [2048, 8], P('expert'), may hold values from 0 to 63, all different within a row; in each aligned block of 128 rows (0 to 127, 128 to 255, ...) at most 32 rows name the same one
- gate_weight: float32 [2048, 8], P('expert'), may hold values from 0.1 to 0.6
- w_gate: bfloat16 [16, 3584, 1024], P('expert', 'dp'), may hold values from -0.09375 to 0.09375
- w_up: bfloat16 [16, 3584, 1024], P('expert', 'dp'), may hold values from -0.09375 to 0.09375
- w_down: bfloat16 [16, 1024, 3584], P('expert', None, 'dp'), may hold values from -0.1875 to 0.1875
- grad_out: bfloat16 [2048, 3584], P('expert', 'dp'), may hold values from -6 to 6
Outputs:
- output: bfloat16 [2048, 3584], P('expert', 'dp')
- grad_tokens: bfloat16 [2048, 3584], P('expert', 'dp')
- grad_down: bfloat16 [16, 1024, 3584], P('expert', None, 'dp')
Inputs may be any that keep to these rules, and one draw needn't show every extreme that they name: `expert_ids`: each row names 8 different experts. Among the rows of one device no expert is named by more than 32 rows, and in some device's rows some expert is named by exactly 32 rows.
All inputs are finite; a program needn't handle non-finite values.
Results may differ from a plain program's by a relative error of at most 0.024.
Values may be sent and summed in bfloat16 or wider, within the bound.
A program may use at most 64 MiB of HBM per device.

v0:
```python
import jax
import jax.numpy as jnp
from jax import lax
from jax.sharding import PartitionSpec as P


def dp_sum(part):
    count = lax.axis_size("dp")
    part = part.astype(jnp.bfloat16)
    total = part.astype(jnp.float32)
    for shift in range(1, count):
        moved = lax.ppermute(part, "dp", [(i, (i + shift) % count) for i in range(count)])
        total = total + moved.astype(jnp.float32)
    return total


def local(tokens, expert_ids, gate_weight, w_gate, w_up, w_down, grad_out):
    tok_dev, fanout = expert_ids.shape
    feature_cols = tokens.shape[1]
    experts = lax.axis_size("expert")
    capacity = max(2, min(tok_dev, 2 * tok_dev * fanout // (4 * experts)))
    ids = jnp.arange(experts, dtype=jnp.int32)
    named = expert_ids[None, :, :] == ids[:, None, None]
    hot = jnp.any(named, axis=2)
    gate_of = jnp.sum(jnp.where(named, gate_weight[None, :, :], 0.0), axis=2)
    rows = jnp.arange(tok_dev, dtype=jnp.int32)
    earlier = (rows[:, None] < rows[None, :]).astype(jnp.bfloat16)
    before = jnp.dot(hot.astype(jnp.bfloat16), earlier, preferred_element_type=jnp.float32)
    slot_of = jnp.where(hot, before.astype(jnp.int32), -1)
    placing = slot_of[:, None, :] == jnp.arange(capacity, dtype=jnp.int32)[None, :, None]
    select = placing.astype(jnp.bfloat16).reshape(experts * capacity, tok_dev)
    slot_gate = jnp.sum(jnp.where(placing, gate_of[:, None, :], 0.0), axis=2).reshape(
        experts * capacity
    )
    x_slab = jnp.dot(select, tokens, preferred_element_type=jnp.float32).astype(jnp.bfloat16)
    x_slab = x_slab.reshape(experts, capacity, feature_cols)
    cot_rows = jnp.dot(select, grad_out, preferred_element_type=jnp.float32)
    c_slab = (slot_gate[:, None] * cot_rows).astype(jnp.bfloat16)
    c_slab = c_slab.reshape(experts, capacity, feature_cols)
    gate_mat = w_gate[0]
    up_mat = w_up[0]
    down_mat = w_down[0]
    row_total = experts * capacity
    transposed = (((1,), (1,)), ((), ()))
    arrived = lax.all_to_all(x_slab, "expert", split_axis=0, concat_axis=0, tiled=True)
    x_rows = arrived.reshape(row_total, feature_cols)
    gate_part = jnp.dot(x_rows, gate_mat, preferred_element_type=jnp.float32)
    up_part = jnp.dot(x_rows, up_mat, preferred_element_type=jnp.float32)
    gate_pre = dp_sum(gate_part)
    up_pre = dp_sum(up_part)
    hidden = (jax.nn.silu(gate_pre) * up_pre).astype(jnp.bfloat16)
    out_rows = jnp.dot(hidden, down_mat, preferred_element_type=jnp.float32).astype(jnp.bfloat16)
    gate_pre, up_pre, hidden, out_rows = (
        gate_pre,
        up_pre,
        hidden,
        out_rows.reshape(experts, capacity, feature_cols),
    )
    back_out = lax.all_to_all(out_rows, "expert", split_axis=0, concat_axis=0, tiled=True)
    arrived_grads = lax.all_to_all(c_slab, "expert", split_axis=0, concat_axis=0, tiled=True)
    c_rows = arrived_grads.reshape(row_total, feature_cols)
    hidden_part = lax.dot_general(c_rows, down_mat, transposed, preferred_element_type=jnp.float32)
    sig = jax.nn.sigmoid(gate_pre)
    grad_hidden = dp_sum(hidden_part)
    grad_gate = (grad_hidden * up_pre * sig * (1.0 + gate_pre * (1.0 - sig))).astype(jnp.bfloat16)
    grad_up = (grad_hidden * jax.nn.silu(gate_pre)).astype(jnp.bfloat16)
    grad_rows = lax.dot_general(grad_gate, gate_mat, transposed, preferred_element_type=jnp.float32)
    grad_rows = grad_rows + lax.dot_general(
        grad_up, up_mat, transposed, preferred_element_type=jnp.float32
    )
    grad_rows = grad_rows.astype(jnp.bfloat16).reshape(experts, capacity, feature_cols)
    down_grad = lax.dot_general(
        hidden, c_rows, (((0,), (0,)), ((), ())), preferred_element_type=jnp.float32
    )
    grad_rows, down_grad = (grad_rows, down_grad.astype(jnp.bfloat16))
    back_grads = lax.all_to_all(grad_rows, "expert", split_axis=0, concat_axis=0, tiled=True)
    scaled = back_out.reshape(row_total, feature_cols).astype(jnp.float32) * slot_gate[:, None]
    output = jnp.dot(select.T, scaled.astype(jnp.bfloat16), preferred_element_type=jnp.float32)
    output = output.astype(jnp.bfloat16)
    grad_flat = back_grads.reshape(row_total, feature_cols)
    grad_tokens = jnp.dot(select.T, grad_flat, preferred_element_type=jnp.float32).astype(
        jnp.bfloat16
    )
    return (output, grad_tokens, down_grad.reshape(1, down_grad.shape[0], feature_cols))


def solution(mesh):
    return jax.shard_map(
        local,
        mesh=mesh,
        in_specs=(
            P("expert", "dp"),
            P("expert", None),
            P("expert", None),
            P("expert", "dp", None),
            P("expert", "dp", None),
            P("expert", None, "dp"),
            P("expert", "dp"),
        ),
        out_specs=(P("expert", "dp"), P("expert", "dp"), P("expert", None, "dp")),
        check_vma=False,
    )
```

profile of v0, /device:TPU:15, one launch (start us, length us, event | category | flops | bytes accessed | tf_op | source)
XLA Modules:
  0.0 262.5 jit_solution(12682456211212196916)
XLA Ops:
  0.6 0.0 copy-start
  0.6 0.8 fusion.36
  1.4 0.1 fusion.31
  1.6 0.7 select_reduce_fusion.1
  2.3 0.1 select_reduce_fusion
  2.4 0.1 mul.46
  2.5 0.1 eq.46
  2.6 0.1 bitcast_compare_fusion
  2.7 0.0 copy-done
  2.8 1.9 multiply_convert_fusion
  4.7 0.0 copy-start.7
  4.7 6.7 %all-to-all-start.2 = ((bf16[16,32,1792]{2,1,0:T(8,128)(2,1)}), bf16[16,32,1792]{2,1,0:T(8,128)(2,1)S(1)}, u32[]{:S(2)}, u32[]{:S(2)}) async-start(bf16[16,32,1792]{2,1,0:T(8,128)(2,1)} %bitcast.8), calls=%async_computation.2 | async-start | bytes 3670016 | tf_op jit(solution)/shard_map/all_to_all | solution.py:60
  11.3 0.0 copy-done.7
  11.3 1.9 convolution_convert_fusion.1
  13.2 39.9 %all-to-all-done.2 = bf16[16,32,1792]{2,1,0:T(8,128)(2,1)S(1)} async-done(((bf16[16,32,1792]{2,1,0:T(8,128)(2,1)}), bf16[16,32,1792]{2,1,0:T(8,128)(2,1)S(1)}, u32[]{:S(2)}, u32[]{:S(2)}) %all-to-all-start.2) | async-done | bytes 1835040 | tf_op jit(solution)/shard_map/all_to_all | solution.py:60
  53.1 0.0 copy-start.1
  53.1 4.8 %all-to-all-start = ((bf16[16,32,1792]{2,1,0:T(8,128)(2,1)}), bf16[16,32,1792]{2,1,0:T(8,128)(2,1)}, u32[]{:S(2)}, u32[]{:S(2)}) async-start(bf16[16,32,1792]{2,1,0:T(8,128)(2,1)} %bitcast.1), calls=%async_computation | async-start | bytes 3670016 | tf_op jit(solution)/shard_map/all_to_all | solution.py:45
  57.9 4.1 %fusion.28 = bf16[512,1024]{1,0:T(8,128)(2,1)S(1)} fusion(bf16[512,1792]{1,0:T(8,128)(2,1)S(1)} %bitcast.55, bf16[1,1024,1792]{2,1,0:T(8,128)(2,1)} %param.12), kind=kOutput, calls=%fused_computation.34 | convolution fusion | flops 1879572480 | bytes 6553600 | tf_op jit(solution)/shard_map/dot_general | solution.py:62
  62.0 0.0 copy-done.1
  62.0 0.3 collective-permute-start.2
  62.3 37.5 %all-to-all-done = bf16[16,32,1792]{2,1,0:T(8,128)(2,1)} async-done(((bf16[16,32,1792]{2,1,0:T(8,128)(2,1)}), bf16[16,32,1792]{2,1,0:T(8,128)(2,1)}, u32[]{:S(2)}, u32[]{:S(2)}) %all-to-all-start) | async-done | bytes 1835040 | tf_op jit(solution)/shard_map/all_to_all | solution.py:45
  99.8 0.0 copy-start.9
  99.8 4.8 %fusion.22 = bf16[512,1024]{1,0:T(8,128)(2,1)S(1)} fusion(bf16[512,1792]{1,0:T(8,128)(2,1)} %bitcast.2, bf16[1,1792,1024]{2,1,0:T(8,128)(2,1)} %param.10), kind=kOutput, calls=%fused_computation.32 | convolution fusion | flops 1879572480 | bytes 6553600 | tf_op jit(solution)/shard_map/dot_general | solution.py:47
  104.6 0.0 copy-done.9
  104.6 0.0 copy-start.8
  104.6 3.7 %fusion.25 = bf16[512,1024]{1,0:T(8,128)(2,1)S(1)} fusion(bf16[512,1792]{1,0:T(8,128)(2,1)} %bitcast.2, bf16[1,1792,1024]{2,1,0:T(8,128)(2,1)S(1)} %copy-done.9), kind=kOutput, calls=%fused_computation.33 | convolution fusion | flops 1879572480 | bytes 6553600 | tf_op jit(solution)/shard_map/dot_general | solution.py:48
  108.4 0.0 copy-start.2
  108.4 0.3 collective-permute-start.1
  108.7 1.2 collective-permute-start
  109.9 0.0 collective-permute-done.2
  109.9 23.1 %collective-permute-done.1 = bf16[512,1024]{1,0:T(8,128)(2,1)S(1)} collective-permute-done((bf16[512,1024]{1,0:T(8,128)(2,1)S(1)}, bf16[512,1024]{1,0:T(8,128)(2,1)S(1)}, u32[]{:S(2)}, u32[]{:S(2)}) %collective-permute-start.1) | collective-permute-done | bytes 1048608 | tf_op jit(solution)/shard_map/ppermute | solution.py:12
  133.1 0.0 copy-start.3
  133.1 22.5 %collective-permute-done = bf16[512,1024]{1,0:T(8,128)(2,1)S(1)} collective-permute-done((bf16[512,1024]{1,0:T(8,128)(2,1)S(1)}, bf16[512,1024]{1,0:T(8,128)(2,1)S(1)}, u32[]{:S(2)}, u32[]{:S(2)}) %collective-permute-start) | collective-permute-done | bytes 1048608 | tf_op jit(solution)/shard_map/ppermute | solution.py:12
  155.5 0.0 copy-done.2
  155.5 0.0 copy-done.3
  155.5 0.0 copy-done.8
  155.5 0.0 copy-start.4
  155.6 4.8 %fusion.8 = f32[512,1792]{1,0:T(8,128)S(1)} fusion(bf16[1,1792,1024]{2,1,0:T(8,128)(2,1)S(1)} %copy-done.8, bf16[512,1024]{1,0:T(8,128)(2,1)S(1)} %collective-permute-done, bf16[512,1024]{1,0:T(8,128)(2,1)S(1)} %fusion.22, bf16[512,1024]{1,0:T(8,128)(2,1)S(1)} %collective-permute-done.1, bf16[512,1024]{1,0:T(8,128)(2,1)S(1)} %fusion.25, ...), kind=kOutput, calls=%fused_computation.9 | convolution fusion | flops 1889009664 | bytes 13631488 | tf_op jit(solution)/shard_map/dot_general | solution.py:67
  160.4 0.0 copy-done.4
  160.4 5.2 %add_convert_fusion = bf16[512,1792]{1,0:T(8,128)(2,1)} fusion(f32[512,1792]{1,0:T(8,128)S(1)} %fusion.8, bf16[1,1792,1024]{2,1,0:T(8,128)(2,1)S(1)} %copy-done.9, bf16[512,1024]{1,0:T(8,128)(2,1)} %collective-permute-done.2, bf16[512,1024]{1,0:T(8,128)(2,1)S(1)} %fusion.28, bf16[512,1024]{1,0:T(8,128)(2,1)S(1)} %collective-permute-done, ...), kind=kOutput, calls=%fused_computation.13 | convolution fusion | flops 1887174656 | bytes 13369344 | tf_op jit(solution)/shard_map/dot_general | solution.py:68
  165.6 5.6 %all-to-all-start.3 = ((bf16[16,32,1792]{2,1,0:T(8,128)(2,1)}), bf16[16,32,1792]{2,1,0:T(8,128)(2,1)S(1)}, u32[]{:S(2)}, u32[]{:S(2)}) async-start(bf16[16,32,1792]{2,1,0:T(8,128)(2,1)} %bitcast.58), calls=%async_computation.3 | async-start | bytes 3670016 | tf_op jit(solution)/shard_map/all_to_all | solution.py:76
  171.2 0.0 copy-start.10
  171.2 3.0 %multiply_convert_fusion.4 = bf16[512,1024]{1,0:T(8,128)(2,1)S(1)} fusion(bf16[512,1024]{1,0:T(8,128)(2,1)} %copy-done.3, bf16[512,1024]{1,0:T(8,128)(2,1)} %copy-done.2, bf16[512,1024]{1,0:T(8,128)(2,1)} %copy-done.4, bf16[512,1024]{1,0:T(8,128)(2,1)S(1)} %fusion.22), kind=kLoop, calls=%fused_computation.26 | loop fusion | flops 6291456 | bytes 5242880 | tf_op jit(solution)/shard_map/convert_element_type | solution.py:51
  174.2 0.0 copy-start.5
  174.3 1.0 copy-done.5
  175.2 0.0 copy-done.10
  175.2 3.3 %fusion.15 = bf16[512,1792]{1,0:T(8,128)(2,1)} fusion(bf16[512,1024]{1,0:T(8,128)(2,1)S(1)} %multiply_convert_fusion.4, bf16[1,1024,1792]{2,1,0:T(8,128)(2,1)S(1)} %copy-done.10), kind=kOutput, calls=%fused_computation.17 | convolution fusion | flops 1879965696 | bytes 6553600 | tf_op jit(solution)/shard_map/dot_general | solution.py:52
  178.6 0.0 copy-start.6
  178.6 34.4 %all-to-all-done.3 = bf16[16,32,1792]{2,1,0:T(8,128)(2,1)S(1)} async-done(((bf16[16,32,1792]{2,1,0:T(8,128)(2,1)}), bf16[16,32,1792]{2,1,0:T(8,128)(2,1)S(1)}, u32[]{:S(2)}, u32[]{:S(2)}) %all-to-all-start.3) | async-done | bytes 1835040 | tf_op jit(solution)/shard_map/all_to_all | solution.py:76
  213.0 4.8 %all-to-all-start.1 = ((bf16[16,32,1792]{2,1,0:T(8,128)(2,1)}), bf16[16,32,1792]{2,1,0:T(8,128)(2,1)}, u32[]{:S(2)}, u32[]{:S(2)}) async-start(bf16[16,32,1792]{2,1,0:T(8,128)(2,1)} %bitcast.57), calls=%async_computation.1 | async-start | bytes 3670016 | tf_op jit(solution)/shard_map/all_to_all | solution.py:59
  217.8 0.0 copy-done.6
  217.8 5.5 %fusion.12 = bf16[1,1024,1792]{2,1,0:T(8,128)(2,1)} fusion(bf16[512,1024]{1,0:T(8,128)(2,1)S(1)} %copy-done.6, bf16[512,1792]{1,0:T(8,128)(2,1)} %bitcast.56), kind=kOutput, calls=%fused_computation.16 | convolution fusion | flops 1880883200 | bytes 6553600 | tf_op jit(solution)/shard_map/dot_general | solution.py:72
  223.2 1.2 fusion.19
  224.4 35.2 %all-to-all-done.1 = bf16[16,32,1792]{2,1,0:T(8,128)(2,1)} async-done(((bf16[16,32,1792]{2,1,0:T(8,128)(2,1)}), bf16[16,32,1792]{2,1,0:T(8,128)(2,1)}, u32[]{:S(2)}, u32[]{:S(2)}) %all-to-all-start.1) | async-done | bytes 1835040 | tf_op jit(solution)/shard_map/all_to_all | solution.py:59
  259.7 2.8 %fusion.18 = bf16[128,1792]{1,0:T(8,128)(2,1)} fusion(bf16[16,32,1792]{2,1,0:T(8,128)(2,1)} %all-to-all-done.1, f32[16,32]{1,0:T(8,128)S(1)} %select_reduce_fusion, s32[16,128]{1,0:T(8,128)S(1)} %fusion.31), kind=kOutput, calls=%fused_computation.21 | convolution fusion | flops 237928448 | bytes 2304000 | tf_op jit(solution)/shard_map/dot_general | solution.py:78
  (1 shorter events, 0.0 us)
Async XLA Ops:
  0.6 2.1 copy-start
  4.7 6.7 %copy-start.7 = (bf16[128,1792]{1,0:T(8,128)(2,1)S(1)}, bf16[128,1792]{1,0:T(8,128)(2,1)}, u32[]{:S(2)}) copy-start(bf16[128,1792]{1,0:T(8,128)(2,1)} %param.7) | copy-start | bytes 1376260
  4.7 48.5 %all-to-all-start.2 = ((bf16[16,32,1792]{2,1,0:T(8,128)(2,1)}), bf16[16,32,1792]{2,1,0:T(8,128)(2,1)S(1)}, u32[]{:S(2)}, u32[]{:S(2)}) async-start(bf16[16,32,1792]{2,1,0:T(8,128)(2,1)} %bitcast.8), calls=%async_computation.2 | async-start | bytes 3670016 | tf_op jit(solution)/shard_map/all_to_all | solution.py:60
  53.1 8.9 %copy-start.1 = (bf16[16,32,1792]{2,1,0:T(8,128)(2,1)}, bf16[16,32,1792]{2,1,0:T(8,128)(2,1)S(1)}, u32[]{:S(2)}) copy-start(bf16[16,32,1792]{2,1,0:T(8,128)(2,1)S(1)} %all-to-all-done.2) | copy-start | bytes 5505028
  53.1 46.7 %all-to-all-start = ((bf16[16,32,1792]{2,1,0:T(8,128)(2,1)}), bf16[16,32,1792]{2,1,0:T(8,128)(2,1)}, u32[]{:S(2)}, u32[]{:S(2)}) async-start(bf16[16,32,1792]{2,1,0:T(8,128)(2,1)} %bitcast.1), calls=%async_computation | async-start | bytes 3670016 | tf_op jit(solution)/shard_map/all_to_all | solution.py:45
  62.0 47.9 %collective-permute-start.2 = (bf16[512,1024]{1,0:T(8,128)(2,1)S(1)}, bf16[512,1024]{1,0:T(8,128)(2,1)}, u32[]{:S(2)}, u32[]{:S(2)}) collective-permute-start(bf16[512,1024]{1,0:T(8,128)(2,1)S(1)} %fusion.28), channel_id=1, source_target_pairs={{0,16},{16,0},{1,17},{17,1},{2,18},{18,2},{3,19},{19,3},{4,20},{20... | collective-permute-start | bytes 3145736 | tf_op jit(solution)/shard_map/ppermute | solution.py:12
  99.8 4.8 %copy-start.9 = (bf16[1,1792,1024]{2,1,0:T(8,128)(2,1)S(1)}, bf16[1,1792,1024]{2,1,0:T(8,128)(2,1)}, u32[]{:S(2)}) copy-start(bf16[1,1792,1024]{2,1,0:T(8,128)(2,1)} %param.11) | copy-start | bytes 11010052
  104.6 50.9 %copy-start.8 = (bf16[1,1792,1024]{2,1,0:T(8,128)(2,1)S(1)}, bf16[1,1792,1024]{2,1,0:T(8,128)(2,1)}, u32[]{:S(2)}) copy-start(bf16[1,1792,1024]{2,1,0:T(8,128)(2,1)} %param.10) | copy-start | bytes 11010052
  108.4 47.2 %copy-start.2 = (bf16[512,1024]{1,0:T(8,128)(2,1)}, bf16[512,1024]{1,0:T(8,128)(2,1)S(1)}, u32[]{:S(2)}) copy-start(bf16[512,1024]{1,0:T(8,128)(2,1)S(1)} %fusion.25) | copy-start | bytes 3145732
  108.4 24.7 %collective-permute-start.1 = (bf16[512,1024]{1,0:T(8,128)(2,1)S(1)}, bf16[512,1024]{1,0:T(8,128)(2,1)S(1)}, u32[]{:S(2)}, u32[]{:S(2)}) collective-permute-start(bf16[512,1024]{1,0:T(8,128)(2,1)S(1)} %fusion.25), channel_id=1, source_target_pairs={{0,16},{16,0},{1,17},{17,1},{2,18},{18,2},{3,19},{19,3},{4,20},{20... | collective-permute-start | bytes 3145736 | tf_op jit(solution)/shard_map/ppermute | solution.py:12
  108.7 46.9 %collective-permute-start = (bf16[512,1024]{1,0:T(8,128)(2,1)S(1)}, bf16[512,1024]{1,0:T(8,128)(2,1)S(1)}, u32[]{:S(2)}, u32[]{:S(2)}) collective-permute-start(bf16[512,1024]{1,0:T(8,128)(2,1)S(1)} %fusion.22), channel_id=1, source_target_pairs={{0,16},{16,0},{1,17},{17,1},{2,18},{18,2},{3,19},{19,3},{4,20},{20... | collective-permute-start | bytes 3145736 | tf_op jit(solution)/shard_map/ppermute | solution.py:12
  133.1 22.5 %copy-start.3 = (bf16[512,1024]{1,0:T(8,128)(2,1)}, bf16[512,1024]{1,0:T(8,128)(2,1)S(1)}, u32[]{:S(2)}) copy-start(bf16[512,1024]{1,0:T(8,128)(2,1)S(1)} %collective-permute-done.1) | copy-start | bytes 3145732
  155.5 4.8 %copy-start.4 = (bf16[512,1024]{1,0:T(8,128)(2,1)}, bf16[512,1024]{1,0:T(8,128)(2,1)S(1)}, u32[]{:S(2)}) copy-start(bf16[512,1024]{1,0:T(8,128)(2,1)S(1)} %collective-permute-done) | copy-start | bytes 3145732
  165.6 47.4 %all-to-all-start.3 = ((bf16[16,32,1792]{2,1,0:T(8,128)(2,1)}), bf16[16,32,1792]{2,1,0:T(8,128)(2,1)S(1)}, u32[]{:S(2)}, u32[]{:S(2)}) async-start(bf16[16,32,1792]{2,1,0:T(8,128)(2,1)} %bitcast.58), calls=%async_computation.3 | async-start | bytes 3670016 | tf_op jit(solution)/shard_map/all_to_all | solution.py:76
  171.2 4.0 %copy-start.10 = (bf16[1,1024,1792]{2,1,0:T(8,128)(2,1)S(1)}, bf16[1,1024,1792]{2,1,0:T(8,128)(2,1)}, u32[]{:S(2)}) copy-start(bf16[1,1024,1792]{2,1,0:T(8,128)(2,1)} %param.12) | copy-start | bytes 11010052
  174.2 1.0 copy-start.5
  178.6 39.2 %copy-start.6 = (bf16[512,1024]{1,0:T(8,128)(2,1)S(1)}, bf16[512,1024]{1,0:T(8,128)(2,1)}, u32[]{:S(2)}) copy-start(bf16[512,1024]{1,0:T(8,128)(2,1)} %copy-done.5) | copy-start | bytes 3145732
  213.0 46.7 %all-to-all-start.1 = ((bf16[16,32,1792]{2,1,0:T(8,128)(2,1)}), bf16[16,32,1792]{2,1,0:T(8,128)(2,1)}, u32[]{:S(2)}, u32[]{:S(2)}) async-start(bf16[16,32,1792]{2,1,0:T(8,128)(2,1)} %bitcast.57), calls=%async_computation.1 | async-start | bytes 3670016 | tf_op jit(solution)/shard_map/all_to_all | solution.py:59
where the time goes:
time: 263 us
  waiting for transfers between devices  193 us (73%)
  matrix products  39.4 us (15%)
  starting transfers between devices  23.7 us (9%)
  other arithmetic  4.83 us (2%)
    ppermute x3, waiting for transfers between devices, dp_sum(): lax.ppermute(part, 'dp', [(i, (i + shift) % count) for i in range(count)])  45.6 us
    all_to_all x1, waiting for transfers between devices, local(): lax.all_to_all(c_slab, 'expert', split_axis=0, concat_axis=0, tiled=True)  39.9 us
    all_to_all x1, waiting for transfers between devices, local(): lax.all_to_all(x_slab, 'expert', split_axis=0, concat_axis=0, tiled=True)  37.5 us
    all_to_all x1, waiting for transfers between devices, local(): lax.all_to_all(out_rows, 'expert', split_axis=0, concat_axis=0, tiled=True)  35.2 us
    all_to_all x1, waiting for transfers between devices, local(): lax.all_to_all(grad_rows, 'expert', split_axis=0, concat_axis=0, tiled=True)  34.4 us
    all_to_all x1, starting transfers between devices, local(): lax.all_to_all(c_slab, 'expert', split_axis=0, concat_axis=0, tiled=True)  6.65 us
    all_to_all x1, starting transfers between devices, local(): lax.all_to_all(grad_rows, 'expert', split_axis=0, concat_axis=0, tiled=True)  5.63 us
    dot_general x1, matrix products, local(): lax.dot_general(hidden, c_rows, (((0,), (0,)), ((), ())), preferred_eleme...  5.45 us
  transfers between devices with their start and end apart: 7, of which 6 were waited for; matrix products, arithmetic and copies ran while one was open for 11% of the time, Pallas kernels for 0%

commit v1 on v0

--- a/solution.py
+++ b/solution.py
@@ -2,6 +2,29 @@
 import jax.numpy as jnp
 from jax import lax
 from jax.sharding import PartitionSpec as P
+
+
+def split_up(value, dim, count):
+    shape = value.shape
+    blocks = value.reshape(*shape[:dim], count, shape[dim] // count, *shape[dim + 1 :])
+    return jnp.moveaxis(blocks, dim, 0)
+
+
+def laid_out(blocks, dim):
+    lengths = list(blocks.shape[1:])
+    lengths[dim] *= blocks.shape[0]
+    return jnp.moveaxis(blocks, 0, dim).reshape(lengths)
+
+
+def sent_to_each(x, axis, split_dim, concat_dim):
+    size, index = (lax.axis_size(axis), lax.axis_index(axis))
+    blocks = split_up(x, split_dim, size)
+    outs = [blocks[index]]
+    for step in range(1, size):
+        sent = blocks[(index + step) % size]
+        outs.append(lax.ppermute(sent, axis, [(i, (i + step) % size) for i in range(size)]))
+    blocks = jnp.stack(outs)[(index - jnp.arange(size)) % size]
+    return laid_out(blocks, concat_dim)
 
 
 def dp_sum(part):
@@ -42,7 +65,7 @@
     down_mat = w_down[0]
     row_total = experts * capacity
     transposed = (((1,), (1,)), ((), ()))
-    arrived = lax.all_to_all(x_slab, "expert", split_axis=0, concat_axis=0, tiled=True)
+    arrived = sent_to_each(x_slab, "expert", 0, 0)
     x_rows = arrived.reshape(row_total, feature_cols)
     gate_part = jnp.dot(x_rows, gate_mat, preferred_element_type=jnp.float32)
     up_part = jnp.dot(x_rows, up_mat, preferred_element_type=jnp.float32)

time: 263 us -> 283 us (1.076)
  starting transfers between devices: 23.7 us -> 54.6 us
  waiting for transfers between devices: 193 us -> 176 us
  local copies, waits for them, and re-layouts: 1.18 us -> 15.3 us
  matrix products: 39.4 us -> 32.6 us
    ppermute x0 -> x15, waiting for transfers between devices: none -> 68.5 us  [sent_to_each(): lax.ppermute(sent, axis, [(i, (i + step) % size) for i in range(size)])]
    all_to_all x1, waiting for transfers between devices: 39.9 us -> 0.01 us  [local(): lax.all_to_all(c_slab, 'expert', split_axis=0, concat_axis=0, tiled=True)]
    all_to_all x1 -> x0, waiting for transfers between devices: 37.5 us -> none  [local(): lax.all_to_all(x_slab, 'expert', split_axis=0, concat_axis=0, tiled=True)]
    ppermute x0 -> x15, starting transfers between devices: none -> 32.3 us  [sent_to_each(): lax.ppermute(sent, axis, [(i, (i + step) % size) for i in range(size)])]
    all_to_all x1, waiting for transfers between devices: 35.2 us -> 5.28 us  [local(): lax.all_to_all(out_rows, 'expert', split_axis=0, concat_axis=0, tiled=True)]
    ppermute x3, waiting for transfers between devices: 45.6 us -> 67.8 us  [dp_sum(): lax.ppermute(part, 'dp', [(i, (i + shift) % count) for i in range(count)])]
    unnamed x22 -> x46, local copies, waits for them, and re-layouts: 1.02 us -> 11.5 us
    all_to_all x1 -> x0, starting transfers between devices: 4.78 us -> none  [local(): lax.all_to_all(x_slab, 'expert', split_axis=0, concat_axis=0, tiled=True)]
  transfers between devices with their start and end apart: 7 -> 21, of which waited for: 6 -> 16; matrix products, arithmetic and copies ran while one was open for 11% -> 15% of each run, Pallas kernels for 0% -> 0%
where the time goes in v1:
time: 283 us
  waiting for transfers between devices  176 us (62%)
  starting transfers between devices  54.6 us (19%)
  matrix products  32.6 us (12%)
  local copies, waits for them, and re-layouts  15.3 us (5%)
  other arithmetic  2.86 us (1%)
    ppermute x15, waiting for transfers between devices, sent_to_each(): lax.ppermute(sent, axis, [(i, (i + step) % size) for i in range(size)])  68.5 us
    ppermute x3, waiting for transfers between devices, dp_sum(): lax.ppermute(part, 'dp', [(i, (i + shift) % count) for i in range(count)])  67.8 us
    all_to_all x1, waiting for transfers between devices, local(): lax.all_to_all(grad_rows, 'expert', split_axis=0, concat_axis=0, tiled=True)  34.8 us
    ppermute x15, starting transfers between devices, sent_to_each(): lax.ppermute(sent, axis, [(i, (i + step) % size) for i in range(size)])  32.3 us
    unnamed x46, local copies, waits for them, and re-layouts  11.5 us
    all_to_all x1, starting transfers between devices, local(): lax.all_to_all(out_rows, 'expert', split_axis=0, concat_axis=0, tiled=True)  9.08 us
    all_to_all x1, starting transfers between devices, local(): lax.all_to_all(c_slab, 'expert', split_axis=0, concat_axis=0, tiled=True)  6.65 us
  transfers between devices with their start and end apart: 21, of which 16 were waited for; matrix products, arithmetic and copies ran while one was open for 15% of the time, Pallas kernels for 0%

profile of v1, /device:TPU:15, one launch (start us, length us, event | category | flops | bytes accessed | tf_op | source)
XLA Modules:
  0.0 282.8 jit_solution(7573314023753940953)
XLA Ops:
  0.6 0.8 fusion.36
  1.6 0.7 select_reduce_fusion.1
  2.8 1.9 multiply_convert_fusion
  4.7 6.7 %all-to-all-start.1 = ((bf16[16,32,1792]{2,1,0:T(8,128)(2,1)}), bf16[16,32,1792]{2,1,0:T(8,128)(2,1)}, u32[]{:S(2)}, u32[]{:S(2)}) async-start(bf16[16,32,1792]{2,1,0:T(8,128)(2,1)} %bitcast.40), calls=%async_computation.1 | async-start | bytes 3670016 | tf_op jit(solution)/shard_map/all_to_all | solution.py:83
  11.3 0.6 convolution_convert_fusion.1
  12.0 0.9 dynamic-slice_bitcast_fusion
  13.6 1.5 collective-permute-start.12
  15.1 3.2 %collective-permute-start.11 = (bf16[1,32,1792]{2,1,0:T(8,128)(2,1)S(1)}, bf16[1,32,1792]{2,1,0:T(8,128)(2,1)S(1)}, u32[]{:S(2)}, u32[]{:S(2)}) collective-permute-start(bf16[1,32,1792]{2,1,0:T(8,128)(2,1)S(1)} %get-tuple-element.6), channel_id=1, source_target_pairs={{0,12},{1,13},{2,14},{3,15},{4,0},{5,1},{6,2},{7,3},{8,4},{9,5},{1... | collective-permute-start | bytes 344072 | tf_op jit(solution)/shard_map/ppermute | solution.py:25
  18.2 1.3 collective-permute-start
  19.6 36.8 %collective-permute-done = bf16[1,32,1792]{2,1,0:T(8,128)(2,1)S(1)} collective-permute-done((bf16[1,32,1792]{2,1,0:T(8,128)(2,1)S(1)}, bf16[1,32,1792]{2,1,0:T(8,128)(2,1)S(1)}, u32[]{:S(2)}, u32[]{:S(2)}) %collective-permute-start) | collective-permute-done | bytes 114720 | tf_op jit(solution)/shard_map/ppermute | solution.py:25
  56.4 0.7 bitcast_dynamic-update-slice_fusion.14
  57.0 3.0 %collective-permute-done.1 = bf16[1,32,1792]{2,1,0:T(8,128)(2,1)S(1)} collective-permute-done((bf16[1,32,1792]{2,1,0:T(8,128)(2,1)S(1)}, bf16[1,32,1792]{2,1,0:T(8,128)(2,1)S(1)}, u32[]{:S(2)}, u32[]{:S(2)}) %collective-permute-start.1) | collective-permute-done | bytes 114720 | tf_op jit(solution)/shard_map/ppermute | solution.py:25
  60.0 3.1 %collective-permute-start.2 = (bf16[1,32,1792]{2,1,0:T(8,128)(2,1)S(1)}, bf16[1,32,1792]{2,1,0:T(8,128)(2,1)S(1)}, u32[]{:S(2)}, u32[]{:S(2)}) collective-permute-start(bf16[1,32,1792]{2,1,0:T(8,128)(2,1)S(1)} %get-tuple-element.15), channel_id=1, source_target_pairs={{0,3},{1,4},{2,5},{3,6},{4,7},{5,8},{6,9},{7,10},{8,11},{9,12},{10... | collective-permute-start | bytes 344072 | tf_op jit(solution)/shard_map/ppermute | solution.py:25
  63.1 0.7 bitcast_dynamic-update-slice_fusion.13
  63.7 1.9 collective-permute-done.2
  65.7 2.5 collective-permute-start.3
  68.2 0.7 bitcast_dynamic-update-slice_fusion.12
  68.9 1.8 collective-permute-done.3
  70.7 3.2 %collective-permute-start.4 = (bf16[1,32,1792]{2,1,0:T(8,128)(2,1)S(1)}, bf16[1,32,1792]{2,1,0:T(8,128)(2,1)S(1)}, u32[]{:S(2)}, u32[]{:S(2)}) collective-permute-start(bf16[1,32,1792]{2,1,0:T(8,128)(2,1)S(1)} %get-tuple-element.13), channel_id=1, source_target_pairs={{0,5},{1,6},{2,7},{3,8},{4,9},{5,10},{6,11},{7,12},{8,13},{9,14},{... | collective-permute-start | bytes 344072 | tf_op jit(solution)/shard_map/ppermute | solution.py:25
  73.9 0.7 bitcast_dynamic-update-slice_fusion.11
  74.6 3.1 %collective-permute-done.4 = bf16[1,32,1792]{2,1,0:T(8,128)(2,1)S(1)} collective-permute-done((bf16[1,32,1792]{2,1,0:T(8,128)(2,1)S(1)}, bf16[1,32,1792]{2,1,0:T(8,128)(2,1)S(1)}, u32[]{:S(2)}, u32[]{:S(2)}) %collective-permute-start.4) | collective-permute-done | bytes 114720 | tf_op jit(solution)/shard_map/ppermute | solution.py:25
  77.6 1.8 collective-permute-start.5
  79.4 0.7 bitcast_dynamic-update-slice_fusion.10
  80.1 2.1 collective-permute-done.5
  82.2 3.0 %collective-permute-start.6 = (bf16[1,32,1792]{2,1,0:T(8,128)(2,1)S(1)}, bf16[1,32,1792]{2,1,0:T(8,128)(2,1)S(1)}, u32[]{:S(2)}, u32[]{:S(2)}) collective-permute-start(bf16[1,32,1792]{2,1,0:T(8,128)(2,1)S(1)} %get-tuple-element.11), channel_id=1, source_target_pairs={{0,7},{1,8},{2,9},{3,10},{4,11},{5,12},{6,13},{7,14},{8,15},{9,0},... | collective-permute-start | bytes 344072 | tf_op jit(solution)/shard_map/ppermute | solution.py:25
  85.2 0.7 bitcast_dynamic-update-slice_fusion.9
  85.9 5.2 %collective-permute-done.6 = bf16[1,32,1792]{2,1,0:T(8,128)(2,1)S(1)} collective-permute-done((bf16[1,32,1792]{2,1,0:T(8,128)(2,1)S(1)}, bf16[1,32,1792]{2,1,0:T(8,128)(2,1)S(1)}, u32[]{:S(2)}, u32[]{:S(2)}) %collective-permute-start.6) | collective-permute-done | bytes 114720 | tf_op jit(solution)/shard_map/ppermute | solution.py:25
  91.2 0.7 bitcast_dynamic-update-slice_fusion.8
  91.9 4.8 %collective-permute-done.7 = bf16[1,32,1792]{2,1,0:T(8,128)(2,1)S(1)} collective-permute-done((bf16[1,32,1792]{2,1,0:T(8,128)(2,1)S(1)}, bf16[1,32,1792]{2,1,0:T(8,128)(2,1)S(1)}, u32[]{:S(2)}, u32[]{:S(2)}) %collective-permute-start.7) | collective-permute-done | bytes 114720 | tf_op jit(solution)/shard_map/ppermute | solution.py:25
  96.6 5.1 %collective-permute-start.8 = (bf16[1,32,1792]{2,1,0:T(8,128)(2,1)S(1)}, bf16[1,32,1792]{2,1,0:T(8,128)(2,1)S(1)}, u32[]{:S(2)}, u32[]{:S(2)}) collective-permute-start(bf16[1,32,1792]{2,1,0:T(8,128)(2,1)S(1)} %get-tuple-element.9), channel_id=1, source_target_pairs={{0,9},{1,10},{2,11},{3,12},{4,13},{5,14},{6,15},{7,0},{8,1},{9,2},... | collective-permute-start | bytes 344072 | tf_op jit(solution)/shard_map/ppermute | solution.py:25
  101.7 0.7 bitcast_dynamic-update-slice_fusion.7
  102.3 2.3 collective-permute-done.8
  104.6 3.5 %collective-permute-start.9 = (bf16[1,32,1792]{2,1,0:T(8,128)(2,1)S(1)}, bf16[1,32,1792]{2,1,0:T(8,128)(2,1)S(1)}, u32[]{:S(2)}, u32[]{:S(2)}) collective-permute-start(bf16[1,32,1792]{2,1,0:T(8,128)(2,1)S(1)} %get-tuple-element.8), channel_id=1, source_target_pairs={{0,10},{1,11},{2,12},{3,13},{4,14},{5,15},{6,0},{7,1},{8,2},{9,3},... | collective-permute-start | bytes 344072 | tf_op jit(solution)/shard_map/ppermute | solution.py:25
  108.1 0.7 bitcast_dynamic-update-slice_fusion.6
  108.8 4.1 %collective-permute-done.9 = bf16[1,32,1792]{2,1,0:T(8,128)(2,1)S(1)} collective-permute-done((bf16[1,32,1792]{2,1,0:T(8,128)(2,1)S(1)}, bf16[1,32,1792]{2,1,0:T(8,128)(2,1)S(1)}, u32[]{:S(2)}, u32[]{:S(2)}) %collective-permute-start.9) | collective-permute-done | bytes 114720 | tf_op jit(solution)/shard_map/ppermute | solution.py:25
  112.8 3.3 %collective-permute-start.10 = (bf16[1,32,1792]{2,1,0:T(8,128)(2,1)S(1)}, bf16[1,32,1792]{2,1,0:T(8,128)(2,1)S(1)}, u32[]{:S(2)}, u32[]{:S(2)}) collective-permute-start(bf16[1,32,1792]{2,1,0:T(8,128)(2,1)S(1)} %get-tuple-element.7), channel_id=1, source_target_pairs={{0,11},{1,12},{2,13},{3,14},{4,15},{5,0},{6,1},{7,2},{8,3},{9,4},{... | collective-permute-start | bytes 344072 | tf_op jit(solution)/shard_map/ppermute | solution.py:25
  116.1 0.7 bitcast_dynamic-update-slice_fusion.5
  116.8 3.5 %collective-permute-done.10 = bf16[1,32,1792]{2,1,0:T(8,128)(2,1)S(1)} collective-permute-done((bf16[1,32,1792]{2,1,0:T(8,128)(2,1)S(1)}, bf16[1,32,1792]{2,1,0:T(8,128)(2,1)S(1)}, u32[]{:S(2)}, u32[]{:S(2)}) %collective-permute-start.10) | collective-permute-done | bytes 114720 | tf_op jit(solution)/shard_map/ppermute | solution.py:25
  120.3 0.7 bitcast_dynamic-update-slice_fusion.4
  121.0 0.7 bitcast_dynamic-update-slice_fusion.3
  121.6 0.7 bitcast_dynamic-update-slice_fusion.2
  122.3 0.7 bitcast_dynamic-update-slice_fusion.1
  122.9 0.7 bitcast_dynamic-update-slice_fusion
  123.6 2.2 gather_fusion
  125.8 4.2 %fusion.22 = bf16[512,1024]{1,0:T(8,128)(2,1)S(1)} fusion(bf16[512,1792]{1,0:T(8,128)(2,1)S(1)} %bitcast.121, bf16[1,1792,1024]{2,1,0:T(8,128)(2,1)} %param.10), kind=kOutput, calls=%fused_computation.33 | convolution fusion | flops 1879572480 | bytes 6553600 | tf_op jit(solution)/shard_map/dot_general | solution.py:70
  130.1 2.1 fusion.25
  132.5 1.2 collective-permute-start.15
  133.7 23.7 %collective-permute-done.16 = bf16[512,1024]{1,0:T(8,128)(2,1)S(1)} collective-permute-done((bf16[512,1024]{1,0:T(8,128)(2,1)S(1)}, bf16[512,1024]{1,0:T(8,128)(2,1)S(1)}, u32[]{:S(2)}, u32[]{:S(2)}) %collective-permute-start.16) | collective-permute-done | bytes 1048608 | tf_op jit(solution)/shard_map/ppermute | solution.py:35
  157.4 20.0 %collective-permute-done.15 = bf16[512,1024]{1,0:T(8,128)(2,1)S(1)} collective-permute-done((bf16[512,1024]{1,0:T(8,128)(2,1)S(1)}, bf16[512,1024]{1,0:T(8,128)(2,1)S(1)}, u32[]{:S(2)}, u32[]{:S(2)}) %collective-permute-start.15) | collective-permute-done | bytes 1048608 | tf_op jit(solution)/shard_map/ppermute | solution.py:35
  177.4 1.1 multiply_convert_fusion.4
  178.5 1.0 copy-done.3
  179.5 3.3 %fusion.15 = bf16[512,1792]{1,0:T(8,128)(2,1)} fusion(bf16[512,1024]{1,0:T(8,128)(2,1)S(1)} %multiply_convert_fusion.4, bf16[1,1024,1792]{2,1,0:T(8,128)(2,1)S(1)} %copy-done.12), kind=kOutput, calls=%fused_computation.18 | convolution fusion | flops 1879965696 | bytes 6553600 | tf_op jit(solution)/shard_map/dot_general | solution.py:75
  182.8 9.1 %all-to-all-start = ((bf16[16,32,1792]{2,1,0:T(8,128)(2,1)}), bf16[16,32,1792]{2,1,0:T(8,128)(2,1)S(1)}, u32[]{:S(2)}, u32[]{:S(2)}) async-start(bf16[16,32,1792]{2,1,0:T(8,128)(2,1)} %bitcast.119), calls=%async_computation | async-start | bytes 3670016 | tf_op jit(solution)/shard_map/all_to_all | solution.py:82
  191.9 4.8 %fusion.28 = bf16[512,1024]{1,0:T(8,128)(2,1)S(1)} fusion(bf16[512,1792]{1,0:T(8,128)(2,1)} %bitcast.41, bf16[1,1024,1792]{2,1,0:T(8,128)(2,1)} %param.12), kind=kOutput, calls=%fused_computation.35 | convolution fusion | flops 1879572480 | bytes 6553600 | tf_op jit(solution)/shard_map/dot_general | solution.py:85
  197.1 24.1 %collective-permute-done.17 = bf16[512,1024]{1,0:T(8,128)(2,1)S(1)} collective-permute-done((bf16[512,1024]{1,0:T(8,128)(2,1)S(1)}, bf16[512,1024]{1,0:T(8,128)(2,1)S(1)}, u32[]{:S(2)}, u32[]{:S(2)}) %collective-permute-start.17) | collective-permute-done | bytes 1048608 | tf_op jit(solution)/shard_map/ppermute | solution.py:35
  221.2 3.2 %fusion.8 = f32[512,1792]{1,0:T(8,128)S(1)} fusion(bf16[1,1792,1024]{2,1,0:T(8,128)(2,1)S(1)} %copy-done.13, bf16[512,1024]{1,0:T(8,128)(2,1)S(1)} %copy-done.10, bf16[512,1024]{1,0:T(8,128)(2,1)S(1)} %fusion.22, bf16[512,1024]{1,0:T(8,128)(2,1)S(1)} %copy-done.8, bf16[512,1024]{1,0:T(8,128)(2,1)S(1)} %copy-done.6, ...), kind=kOutput, calls=%fused_computation.10 | convolution fusion | flops 1889009664 | bytes 13631488 | tf_op jit(solution)/shard_map/dot_general | solution.py:90
  224.4 4.0 %add_convert_fusion = bf16[512,1792]{1,0:T(8,128)(2,1)} fusion(f32[512,1792]{1,0:T(8,128)S(1)} %fusion.8, bf16[1,1792,1024]{2,1,0:T(8,128)(2,1)S(1)} %copy-done.15, bf16[512,1024]{1,0:T(8,128)(2,1)S(1)} %collective-permute-done.17, bf16[512,1024]{1,0:T(8,128)(2,1)S(1)} %fusion.28, bf16[512,1024]{1,0:T(8,128)(2,1)S(1)} %copy-done.10, ...), kind=kOutput, calls=%fused_computation.14 | convolution fusion | flops 1887174656 | bytes 13369344 | tf_op jit(solution)/shard_map/dot_general | solution.py:91
  228.4 5.3 %all-to-all-done = bf16[16,32,1792]{2,1,0:T(8,128)(2,1)S(1)} async-done(((bf16[16,32,1792]{2,1,0:T(8,128)(2,1)}), bf16[16,32,1792]{2,1,0:T(8,128)(2,1)S(1)}, u32[]{:S(2)}, u32[]{:S(2)}) %all-to-all-start) | async-done | bytes 1835040 | tf_op jit(solution)/shard_map/all_to_all | solution.py:82
  233.7 1.3 copy-done.1
  235.0 4.8 %all-to-all-start.2 = ((bf16[16,32,1792]{2,1,0:T(8,128)(2,1)}), bf16[16,32,1792]{2,1,0:T(8,128)(2,1)S(1)}, u32[]{:S(2)}, u32[]{:S(2)}) async-start(bf16[16,32,1792]{2,1,0:T(8,128)(2,1)} %bitcast.120), calls=%async_computation.2 | async-start | bytes 3670016 | tf_op jit(solution)/shard_map/all_to_all | solution.py:99
  239.8 5.6 %fusion.12 = bf16[1,1024,1792]{2,1,0:T(8,128)(2,1)} fusion(bf16[512,1024]{1,0:T(8,128)(2,1)S(1)} %copy-done.4, bf16[512,1792]{1,0:T(8,128)(2,1)} %bitcast.41), kind=kOutput, calls=%fused_computation.17 | convolution fusion | flops 1880883200 | bytes 6553600 | tf_op jit(solution)/shard_map/dot_general | solution.py:95
  245.3 1.4 fusion.18
  246.7 34.8 %all-to-all-done.2 = bf16[16,32,1792]{2,1,0:T(8,128)(2,1)S(1)} async-done(((bf16[16,32,1792]{2,1,0:T(8,128)(2,1)}), bf16[16,32,1792]{2,1,0:T(8,128)(2,1)S(1)}, u32[]{:S(2)}, u32[]{:S(2)}) %all-to-all-start.2) | async-done | bytes 1835040 | tf_op jit(solution)/shard_map/all_to_all | solution.py:99
  281.5 1.2 fusion.19
  (49 shorter events, 2.1 us)
Async XLA Ops:
  0.6 2.1 copy-start
  4.7 6.7 %copy-start.11 = (bf16[128,1792]{1,0:T(8,128)(2,1)S(1)}, bf16[128,1792]{1,0:T(8,128)(2,1)}, u32[]{:S(2)}) copy-start(bf16[128,1792]{1,0:T(8,128)(2,1)} %param.7) | copy-start | bytes 1376260
  4.7 178.1 %all-to-all-start.1 = ((bf16[16,32,1792]{2,1,0:T(8,128)(2,1)}), bf16[16,32,1792]{2,1,0:T(8,128)(2,1)}, u32[]{:S(2)}, u32[]{:S(2)}) async-start(bf16[16,32,1792]{2,1,0:T(8,128)(2,1)} %bitcast.40), calls=%async_computation.1 | async-start | bytes 3670016 | tf_op jit(solution)/shard_map/all_to_all | solution.py:83
  12.9 110.0 %collective-permute-start.14 = (bf16[1,32,1792]{2,1,0:T(8,128)(2,1)S(1)}, bf16[1,32,1792]{2,1,0:T(8,128)(2,1)S(1)}, u32[]{:S(2)}, u32[]{:S(2)}) collective-permute-start(bf16[1,32,1792]{2,1,0:T(8,128)(2,1)S(1)} %get-tuple-element.3), channel_id=1, source_target_pairs={{0,15},{1,0},{2,1},{3,2},{4,3},{5,4},{6,5},{7,6},{8,7},{9,8},{10,9... | collective-permute-start | bytes 344072 | tf_op jit(solution)/shard_map/ppermute | solution.py:25
  13.3 108.9 %collective-permute-start.13 = (bf16[1,32,1792]{2,1,0:T(8,128)(2,1)S(1)}, bf16[1,32,1792]{2,1,0:T(8,128)(2,1)S(1)}, u32[]{:S(2)}, u32[]{:S(2)}) collective-permute-start(bf16[1,32,1792]{2,1,0:T(8,128)(2,1)S(1)} %get-tuple-element.4), channel_id=1, source_target_pairs={{0,14},{1,15},{2,0},{3,1},{4,2},{5,3},{6,4},{7,5},{8,6},{9,7},{10,... | collective-permute-start | bytes 344072 | tf_op jit(solution)/shard_map/ppermute | solution.py:25
  13.6 108.0 %collective-permute-start.12 = (bf16[1,32,1792]{2,1,0:T(8,128)(2,1)S(1)}, bf16[1,32,1792]{2,1,0:T(8,128)(2,1)S(1)}, u32[]{:S(2)}, u32[]{:S(2)}) collective-permute-start(bf16[1,32,1792]{2,1,0:T(8,128)(2,1)S(1)} %get-tuple-element.5), channel_id=1, source_target_pairs={{0,13},{1,14},{2,15},{3,0},{4,1},{5,2},{6,3},{7,4},{8,5},{9,6},{10... | collective-permute-start | bytes 344072 | tf_op jit(solution)/shard_map/ppermute | solution.py:25
  15.1 105.9 %collective-permute-start.11 = (bf16[1,32,1792]{2,1,0:T(8,128)(2,1)S(1)}, bf16[1,32,1792]{2,1,0:T(8,128)(2,1)S(1)}, u32[]{:S(2)}, u32[]{:S(2)}) collective-permute-start(bf16[1,32,1792]{2,1,0:T(8,128)(2,1)S(1)} %get-tuple-element.6), channel_id=1, source_target_pairs={{0,12},{1,13},{2,14},{3,15},{4,0},{5,1},{6,2},{7,3},{8,4},{9,5},{1... | collective-permute-start | bytes 344072 | tf_op jit(solution)/shard_map/ppermute | solution.py:25
  18.2 38.1 %collective-permute-start = (bf16[1,32,1792]{2,1,0:T(8,128)(2,1)S(1)}, bf16[1,32,1792]{2,1,0:T(8,128)(2,1)S(1)}, u32[]{:S(2)}, u32[]{:S(2)}) collective-permute-start(bf16[1,32,1792]{2,1,0:T(8,128)(2,1)S(1)} %get-tuple-element.17), channel_id=1, source_target_pairs={{0,1},{1,2},{2,3},{3,4},{4,5},{5,6},{6,7},{7,8},{8,9},{9,10},{10,1... | collective-permute-start | bytes 344072 | tf_op jit(solution)/shard_map/ppermute | solution.py:25
  56.4 3.6 %collective-permute-start.1 = (bf16[1,32,1792]{2,1,0:T(8,128)(2,1)S(1)}, bf16[1,32,1792]{2,1,0:T(8,128)(2,1)S(1)}, u32[]{:S(2)}, u32[]{:S(2)}) collective-permute-start(bf16[1,32,1792]{2,1,0:T(8,128)(2,1)S(1)} %get-tuple-element.16), channel_id=1, source_target_pairs={{0,2},{1,3},{2,4},{3,5},{4,6},{5,7},{6,8},{7,9},{8,10},{9,11},{10,... | collective-permute-start | bytes 344072 | tf_op jit(solution)/shard_map/ppermute | solution.py:25
  60.0 5.6 %collective-permute-start.2 = (bf16[1,32,1792]{2,1,0:T(8,128)(2,1)S(1)}, bf16[1,32,1792]{2,1,0:T(8,128)(2,1)S(1)}, u32[]{:S(2)}, u32[]{:S(2)}) collective-permute-start(bf16[1,32,1792]{2,1,0:T(8,128)(2,1)S(1)} %get-tuple-element.15), channel_id=1, source_target_pairs={{0,3},{1,4},{2,5},{3,6},{4,7},{5,8},{6,9},{7,10},{8,11},{9,12},{10... | collective-permute-start | bytes 344072 | tf_op jit(solution)/shard_map/ppermute | solution.py:25
  65.7 5.0 %collective-permute-start.3 = (bf16[1,32,1792]{2,1,0:T(8,128)(2,1)S(1)}, bf16[1,32,1792]{2,1,0:T(8,128)(2,1)S(1)}, u32[]{:S(2)}, u32[]{:S(2)}) collective-permute-start(bf16[1,32,1792]{2,1,0:T(8,128)(2,1)S(1)} %get-tuple-element.14), channel_id=1, source_target_pairs={{0,4},{1,5},{2,6},{3,7},{4,8},{5,9},{6,10},{7,11},{8,12},{9,13},{1... | collective-permute-start | bytes 344072 | tf_op jit(solution)/shard_map/ppermute | solution.py:25
  70.7 7.0 %collective-permute-start.4 = (bf16[1,32,1792]{2,1,0:T(8,128)(2,1)S(1)}, bf16[1,32,1792]{2,1,0:T(8,128)(2,1)S(1)}, u32[]{:S(2)}, u32[]{:S(2)}) collective-permute-start(bf16[1,32,1792]{2,1,0:T(8,128)(2,1)S(1)} %get-tuple-element.13), channel_id=1, source_target_pairs={{0,5},{1,6},{2,7},{3,8},{4,9},{5,10},{6,11},{7,12},{8,13},{9,14},{... | collective-permute-start | bytes 344072 | tf_op jit(solution)/shard_map/ppermute | solution.py:25
  77.6 4.5 %collective-permute-start.5 = (bf16[1,32,1792]{2,1,0:T(8,128)(2,1)S(1)}, bf16[1,32,1792]{2,1,0:T(8,128)(2,1)S(1)}, u32[]{:S(2)}, u32[]{:S(2)}) collective-permute-start(bf16[1,32,1792]{2,1,0:T(8,128)(2,1)S(1)} %get-tuple-element.12), channel_id=1, source_target_pairs={{0,6},{1,7},{2,8},{3,9},{4,10},{5,11},{6,12},{7,13},{8,14},{9,15},... | collective-permute-start | bytes 344072 | tf_op jit(solution)/shard_map/ppermute | solution.py:25
  82.2 8.9 %collective-permute-start.6 = (bf16[1,32,1792]{2,1,0:T(8,128)(2,1)S(1)}, bf16[1,32,1792]{2,1,0:T(8,128)(2,1)S(1)}, u32[]{:S(2)}, u32[]{:S(2)}) collective-permute-start(bf16[1,32,1792]{2,1,0:T(8,128)(2,1)S(1)} %get-tuple-element.11), channel_id=1, source_target_pairs={{0,7},{1,8},{2,9},{3,10},{4,11},{5,12},{6,13},{7,14},{8,15},{9,0},... | collective-permute-start | bytes 344072 | tf_op jit(solution)/shard_map/ppermute | solution.py:25
  91.1 5.6 %collective-permute-start.7 = (bf16[1,32,1792]{2,1,0:T(8,128)(2,1)S(1)}, bf16[1,32,1792]{2,1,0:T(8,128)(2,1)S(1)}, u32[]{:S(2)}, u32[]{:S(2)}) collective-permute-start(bf16[1,32,1792]{2,1,0:T(8,128)(2,1)S(1)} %get-tuple-element.10), channel_id=1, source_target_pairs={{0,8},{1,9},{2,10},{3,11},{4,12},{5,13},{6,14},{7,15},{8,0},{9,1},... | collective-permute-start | bytes 344072 | tf_op jit(solution)/shard_map/ppermute | solution.py:25
  96.6 8.0 %collective-permute-start.8 = (bf16[1,32,1792]{2,1,0:T(8,128)(2,1)S(1)}, bf16[1,32,1792]{2,1,0:T(8,128)(2,1)S(1)}, u32[]{:S(2)}, u32[]{:S(2)}) collective-permute-start(bf16[1,32,1792]{2,1,0:T(8,128)(2,1)S(1)} %get-tuple-element.9), channel_id=1, source_target_pairs={{0,9},{1,10},{2,11},{3,12},{4,13},{5,14},{6,15},{7,0},{8,1},{9,2},... | collective-permute-start | bytes 344072 | tf_op jit(solution)/shard_map/ppermute | solution.py:25
  104.6 8.2 %collective-permute-start.9 = (bf16[1,32,1792]{2,1,0:T(8,128)(2,1)S(1)}, bf16[1,32,1792]{2,1,0:T(8,128)(2,1)S(1)}, u32[]{:S(2)}, u32[]{:S(2)}) collective-permute-start(bf16[1,32,1792]{2,1,0:T(8,128)(2,1)S(1)} %get-tuple-element.8), channel_id=1, source_target_pairs={{0,10},{1,11},{2,12},{3,13},{4,14},{5,15},{6,0},{7,1},{8,2},{9,3},... | collective-permute-start | bytes 344072 | tf_op jit(solution)/shard_map/ppermute | solution.py:25
  112.8 7.5 %collective-permute-start.10 = (bf16[1,32,1792]{2,1,0:T(8,128)(2,1)S(1)}, bf16[1,32,1792]{2,1,0:T(8,128)(2,1)S(1)}, u32[]{:S(2)}, u32[]{:S(2)}) collective-permute-start(bf16[1,32,1792]{2,1,0:T(8,128)(2,1)S(1)} %get-tuple-element.7), channel_id=1, source_target_pairs={{0,11},{1,12},{2,13},{3,14},{4,15},{5,0},{6,1},{7,2},{8,3},{9,4},{... | collective-permute-start | bytes 344072 | tf_op jit(solution)/shard_map/ppermute | solution.py:25
  125.8 4.3 %copy-start.14 = (bf16[1,1792,1024]{2,1,0:T(8,128)(2,1)S(1)}, bf16[1,1792,1024]{2,1,0:T(8,128)(2,1)}, u32[]{:S(2)}) copy-start(bf16[1,1792,1024]{2,1,0:T(8,128)(2,1)} %param.11) | copy-start | bytes 11010052
  132.2 46.3 %copy-start.5 = (bf16[512,1024]{1,0:T(8,128)(2,1)}, bf16[512,1024]{1,0:T(8,128)(2,1)S(1)}, u32[]{:S(2)}) copy-start(bf16[512,1024]{1,0:T(8,128)(2,1)S(1)} %fusion.25) | copy-start | bytes 3145732
  132.2 47.3 %copy-start.12 = (bf16[1,1024,1792]{2,1,0:T(8,128)(2,1)S(1)}, bf16[1,1024,1792]{2,1,0:T(8,128)(2,1)}, u32[]{:S(2)}) copy-start(bf16[1,1024,1792]{2,1,0:T(8,128)(2,1)} %param.12) | copy-start | bytes 11010052
  132.2 25.2 %collective-permute-start.16 = (bf16[512,1024]{1,0:T(8,128)(2,1)S(1)}, bf16[512,1024]{1,0:T(8,128)(2,1)S(1)}, u32[]{:S(2)}, u32[]{:S(2)}) collective-permute-start(bf16[512,1024]{1,0:T(8,128)(2,1)S(1)} %fusion.25), channel_id=1, source_target_pairs={{0,16},{16,0},{1,17},{17,1},{2,18},{18,2},{3,19},{19,3},{4,20},{20... | collective-permute-start | bytes 3145736 | tf_op jit(solution)/shard_map/ppermute | solution.py:35
  132.5 44.9 %collective-permute-start.15 = (bf16[512,1024]{1,0:T(8,128)(2,1)S(1)}, bf16[512,1024]{1,0:T(8,128)(2,1)S(1)}, u32[]{:S(2)}, u32[]{:S(2)}) collective-permute-start(bf16[512,1024]{1,0:T(8,128)(2,1)S(1)} %fusion.22), channel_id=1, source_target_pairs={{0,16},{16,0},{1,17},{17,1},{2,18},{18,2},{3,19},{19,3},{4,20},{20... | collective-permute-start | bytes 3145736 | tf_op jit(solution)/shard_map/ppermute | solution.py:35
  157.4 21.1 %copy-start.7 = (bf16[512,1024]{1,0:T(8,128)(2,1)}, bf16[512,1024]{1,0:T(8,128)(2,1)S(1)}, u32[]{:S(2)}) copy-start(bf16[512,1024]{1,0:T(8,128)(2,1)S(1)} %collective-permute-done.16) | copy-start | bytes 3145732
  177.4 1.1 copy-start.9
  178.5 1.0 copy-start.3
  182.8 50.9 %all-to-all-start = ((bf16[16,32,1792]{2,1,0:T(8,128)(2,1)}), bf16[16,32,1792]{2,1,0:T(8,128)(2,1)S(1)}, u32[]{:S(2)}, u32[]{:S(2)}) async-start(bf16[16,32,1792]{2,1,0:T(8,128)(2,1)} %bitcast.119), calls=%async_computation | async-start | bytes 3670016 | tf_op jit(solution)/shard_map/all_to_all | solution.py:82
  191.9 29.3 %copy-start.6 = (bf16[512,1024]{1,0:T(8,128)(2,1)S(1)}, bf16[512,1024]{1,0:T(8,128)(2,1)}, u32[]{:S(2)}) copy-start(bf16[512,1024]{1,0:T(8,128)(2,1)} %copy-done.5) | copy-start | bytes 3145732
  191.9 29.3 %copy-start.8 = (bf16[512,1024]{1,0:T(8,128)(2,1)S(1)}, bf16[512,1024]{1,0:T(8,128)(2,1)}, u32[]{:S(2)}) copy-start(bf16[512,1024]{1,0:T(8,128)(2,1)} %copy-done.7) | copy-start | bytes 3145732
  191.9 29.3 %copy-start.10 = (bf16[512,1024]{1,0:T(8,128)(2,1)S(1)}, bf16[512,1024]{1,0:T(8,128)(2,1)}, u32[]{:S(2)}) copy-start(bf16[512,1024]{1,0:T(8,128)(2,1)} %copy-done.9) | copy-start | bytes 3145732
  191.9 29.3 %copy-start.13 = (bf16[1,1792,1024]{2,1,0:T(8,128)(2,1)S(1)}, bf16[1,1792,1024]{2,1,0:T(8,128)(2,1)}, u32[]{:S(2)}) copy-start(bf16[1,1792,1024]{2,1,0:T(8,128)(2,1)} %param.10) | copy-start | bytes 11010052
  196.8 27.6 %copy-start.15 = (bf16[1,1792,1024]{2,1,0:T(8,128)(2,1)S(1)}, bf16[1,1792,1024]{2,1,0:T(8,128)(2,1)}, u32[]{:S(2)}) copy-start(bf16[1,1792,1024]{2,1,0:T(8,128)(2,1)} %param.11) | copy-start | bytes 11010052
  196.8 24.4 %collective-permute-start.17 = (bf16[512,1024]{1,0:T(8,128)(2,1)S(1)}, bf16[512,1024]{1,0:T(8,128)(2,1)S(1)}, u32[]{:S(2)}, u32[]{:S(2)}) collective-permute-start(bf16[512,1024]{1,0:T(8,128)(2,1)S(1)} %fusion.28), channel_id=1, source_target_pairs={{0,16},{16,0},{1,17},{17,1},{2,18},{18,2},{3,19},{19,3},{4,20},{20... | collective-permute-start | bytes 3145736 | tf_op jit(solution)/shard_map/ppermute | solution.py:35
  228.4 11.3 %copy-start.4 = (bf16[512,1024]{1,0:T(8,128)(2,1)S(1)}, bf16[512,1024]{1,0:T(8,128)(2,1)}, u32[]{:S(2)}) copy-start(bf16[512,1024]{1,0:T(8,128)(2,1)} %copy-done.3) | copy-start | bytes 3145732
  233.7 1.3 copy-start.1
  235.0 46.6 %all-to-all-start.2 = ((bf16[16,32,1792]{2,1,0:T(8,128)(2,1)}), bf16[16,32,1792]{2,1,0:T(8,128)(2,1)S(1)}, u32[]{:S(2)}, u32[]{:S(2)}) async-start(bf16[16,32,1792]{2,1,0:T(8,128)(2,1)} %bitcast.120), calls=%async_computation.2 | async-start | bytes 3670016 | tf_op jit(solution)/shard_map/all_to_all | solution.py:99
  239.7 5.6 %copy-start.2 = (bf16[16,32,1792]{2,1,0:T(8,128)(2,1)S(1)}, bf16[16,32,1792]{2,1,0:T(8,128)(2,1)}, u32[]{:S(2)}) copy-start(bf16[16,32,1792]{2,1,0:T(8,128)(2,1)} %copy-done.1) | copy-start | bytes 5505028
